TPU v7x, 32 devices: a whole 2x2x4 slice. The times are simulated.
32 devices in a mesh: groups: 2 (over y), expert: 4 (over z), dp: 2 (over x), inner: 2 (over core).
Axes of the slice: x: 2, y: 2, z: 4, core: 2. Of those that a mesh axis runs over, the one named last changes fastest.
Arguments:
- tokens: bfloat16 [2048, 1536], P(('groups', 'expert', 'dp'), 'inner'), parts along dimension 0, may hold values from -6 to 6
- out_grad: bfloat16 [2048, 1536], P(('groups', 'expert', 'dp'), 'inner'), parts along dimension 0, may hold values from -6 to 6
- expert_ids: int32 [2048, 8], P(('groups', 'expert', 'dp')), parts along dimension 0, may hold values from 0 to 63, all different within a row; in each aligned block of 128 rows (0 to 127, 128 to 255, ...) at most 17 rows name the same one
- gate_probs: float32 [2048, 8], P(('groups', 'expert', 'dp')), parts along dimension 0, may hold values from 0.05 to 0.5
- gate_weight: bfloat16 [64, 1536, 384], P('expert', 'inner', 'dp'), may hold values from -0.15625 to 0.15625
- up_weight: bfloat16 [64, 1536, 384], P('expert', 'inner', 'dp'), may hold values from -0.15625 to 0.15625
- down_weight: bfloat16 [64, 384, 1536], P('expert', 'dp', 'inner'), may hold values from -0.3125 to 0.3125
Outputs:
- token_grad: bfloat16 [2048, 1536], P(('groups', 'expert', 'dp'), 'inner'), parts along dimension 0
- prob_grad: float32 [2048, 8], P(('groups', 'expert', 'dp')), parts along dimension 0
- gate_weight_grad: bfloat16 [128, 1536, 384], P(('groups', 'expert'), 'inner', 'dp'), parts along dimension 0
- up_weight_grad: bfloat16 [128, 1536, 384], P(('groups', 'expert'), 'inner', 'dp'), parts along dimension 0
- down_weight_grad: bfloat16 [128, 384, 1536], P(('groups', 'expert'), 'dp', 'inner'), parts along dimension 0
There are 2 independent parts, one for each index of `groups`. A program takes and returns all parts, laid end to end along the dimension named above; an argument that names none is the same for every part. Nothing has to cross between parts.
Inputs may be any that keep to these rules, and one draw needn't show every extreme that they name: `expert_ids`: within the rows of one block of 128 tokens no expert is chosen more than 17 times, and some expert is chosen exactly 17 times in some block; a token's 8 experts differ.
All inputs are finite; a program needn't handle non-finite values.
Results may differ from a plain program's by a relative error of at most 0.015.
Values may be sent and summed in bfloat16 or wider, within the bound.
A program may use at most 192 MiB of HBM per device.

v0:
```python
import jax
import jax.numpy as jnp
from jax import lax
from jax.sharding import PartitionSpec as P


def on_device(tokens, out_grad, expert_ids, gate_probs, gate_weight, up_weight, down_weight):
    tok_rows, width_half = tokens.shape
    top_count = expert_ids.shape[1]
    per_dev = gate_weight.shape[0]
    owners = lax.axis_size("expert")
    experts = per_dev * owners
    capacity = tok_rows * top_count // experts + 1
    row_count = owners * capacity
    total_slots = experts * capacity
    pair_count = tok_rows * top_count
    chosen = expert_ids.reshape(-1)
    matches = (chosen[:, None] == jnp.arange(experts, dtype=jnp.int32)[None, :]).astype(jnp.int32)
    before = jnp.cumsum(matches, axis=0) - matches
    slot_index = jnp.sum(before * matches, axis=1)
    target = chosen % per_dev * row_count + chosen // per_dev * capacity + slot_index
    source_tok = (
        jnp.zeros((total_slots,), jnp.int32)
        .at[target]
        .set(jnp.arange(pair_count, dtype=jnp.int32) // top_count)
    )
    filled = jnp.zeros((total_slots,), jnp.bfloat16).at[target].set(1)
    slot_probs = (
        jnp.zeros((total_slots,), jnp.float32)
        .at[target]
        .set(gate_probs.reshape(-1))
        .astype(jnp.bfloat16)
    )
    sent_rows = (tokens[source_tok] * filled[:, None]).reshape(
        per_dev, owners, capacity, width_half
    )
    sent_grads = (out_grad[source_tok] * filled[:, None]).reshape(
        per_dev, owners, capacity, width_half
    )
    sent_probs = slot_probs.reshape(per_dev, owners, capacity)
    arrived_rows, arrived_grads, arrived_probs = (
        lax.all_to_all(sent_rows, "expert", split_axis=1, concat_axis=1, tiled=True),
        lax.all_to_all(sent_grads, "expert", split_axis=1, concat_axis=1, tiled=True),
        lax.all_to_all(sent_probs, "expert", split_axis=1, concat_axis=1, tiled=True),
    )
    full_gate, full_up, full_down = (
        lax.all_gather(gate_weight, "dp", axis=2, tiled=True),
        lax.all_gather(up_weight, "dp", axis=2, tiled=True),
        lax.all_gather(down_weight, "dp", axis=1, tiled=True),
    )
    expert_rows = arrived_rows.reshape(per_dev, row_count, width_half)
    gate_part = jnp.einsum(
        "jrd,jdf->jrf", expert_rows, full_gate, preferred_element_type=jnp.float32
    )
    up_part = jnp.einsum("jrd,jdf->jrf", expert_rows, full_up, preferred_element_type=jnp.float32)
    gate_sum, up_sum = (
        lax.psum(gate_part.astype(jnp.bfloat16), "inner").astype(jnp.float32),
        lax.psum(up_part.astype(jnp.bfloat16), "inner").astype(jnp.float32),
    )
    sigmoid_gate = jax.nn.sigmoid(gate_sum)
    activated = gate_sum * sigmoid_gate
    hidden = (activated * up_sum).astype(jnp.bfloat16)
    expert_grads = arrived_grads.reshape(per_dev, row_count, width_half)
    prob_col = arrived_probs.reshape(per_dev, row_count, 1).astype(jnp.float32)
    slope_part = jnp.einsum(
        "jrd,jfd->jrf", expert_grads, full_down, preferred_element_type=jnp.float32
    )
    slope_sum = lax.psum(slope_part.astype(jnp.bfloat16), "inner").astype(jnp.float32)
    scores = jnp.sum(hidden.astype(jnp.float32) * slope_sum, axis=-1)
    hidden_grad = prob_col * slope_sum
    gate_back = (
        hidden_grad * up_sum * sigmoid_gate * (1.0 + gate_sum * (1.0 - sigmoid_gate))
    ).astype(jnp.bfloat16)
    up_back = (hidden_grad * activated).astype(jnp.bfloat16)
    row_grads = jnp.einsum("jrf,jdf->jrd", gate_back, full_gate, preferred_element_type=jnp.float32)
    row_grads = (
        row_grads + jnp.einsum("jrf,jdf->jrd", up_back, full_up, preferred_element_type=jnp.float32)
    ).astype(jnp.bfloat16)
    returned_rows, returned_scores = (
        lax.all_to_all(
            row_grads.reshape(per_dev, owners, capacity, width_half),
            "expert",
            split_axis=1,
            concat_axis=1,
            tiled=True,
        ),
        lax.all_to_all(
            scores.astype(jnp.bfloat16).reshape(per_dev, owners, capacity),
            "expert",
            split_axis=1,
            concat_axis=1,
            tiled=True,
        ),
    )
    pair_rows = returned_rows.reshape(total_slots, width_half)[target]
    token_grad = jnp.sum(
        pair_rows.reshape(tok_rows, top_count, width_half).astype(jnp.float32), axis=1
    ).astype(jnp.bfloat16)
    prob_grad = returned_scores.reshape(-1)[target].astype(jnp.float32).reshape(tok_rows, top_count)
    grad_gate = jnp.einsum(
        "jrd,jrf->jdf", expert_rows, gate_back, preferred_element_type=jnp.float32
    )
    grad_up = jnp.einsum("jrd,jrf->jdf", expert_rows, up_back, preferred_element_type=jnp.float32)
    down_rows = (prob_col * expert_grads).astype(jnp.bfloat16)
    grad_down = jnp.einsum("jrf,jrd->jfd", hidden, down_rows, preferred_element_type=jnp.float32)
    summed_gate, summed_up, summed_down = (
        lax.psum_scatter(
            grad_gate.astype(jnp.bfloat16), "dp", scatter_dimension=2, tiled=True
        ).astype(jnp.float32),
        lax.psum_scatter(
            grad_up.astype(jnp.bfloat16), "dp", scatter_dimension=2, tiled=True
        ).astype(jnp.float32),
        lax.psum_scatter(
            grad_down.astype(jnp.bfloat16), "dp", scatter_dimension=1, tiled=True
        ).astype(jnp.float32),
    )
    return (
        token_grad,
        prob_grad,
        summed_gate.astype(jnp.bfloat16),
        summed_up.astype(jnp.bfloat16),
        summed_down.astype(jnp.bfloat16),
    )


def solution(mesh):
    placed = (
        P(("groups", "expert", "dp"), "inner"),
        P(("groups", "expert", "dp"), "inner"),
        P(("groups", "expert", "dp"), None),
        P(("groups", "expert", "dp"), None),
        P("expert", "inner", "dp"),
        P("expert", "inner", "dp"),
        P("expert", "dp", "inner"),
    )
    return jax.shard_map(
        on_device,
        mesh=mesh,
        in_specs=placed,
        out_specs=(
            P(("groups", "expert", "dp"), "inner"),
            P(("groups", "expert", "dp"), None),
            P(("groups", "expert"), "inner", "dp"),
            P(("groups", "expert"), "inner", "dp"),
            P(("groups", "expert"), "dp", "inner"),
        ),
        check_vma=False,
    )
```

profile of v0, /device:TPU:0, one launch (start us, length us, event | category | flops | bytes accessed | tf_op | source)
XLA Modules:
  0.0 753.5 jit_solution(1835674188766818200)
XLA Ops:
  9.8 18.0 %reduce-window.6 = s32[64,8,128]{2,1,0:T(8,128)S(1)} reduce-window(s32[64,8,128]{2,1,0:T(8,128)S(1)} %fusion.24, s32[]{:T(128)} %constant.51.clone.1), window={size=1x1x128 pad=0_0x0_0x127_0}, to_apply=%region_0.0 | reduce-window | flops 8323072 | bytes 524292 | tf_op jit(solution)/shard_map/reduce-window
  28.5 4.3 scatter_custom_fusion.1
  32.9 4.8 gather_fusion.1
  40.2 7.6 %scatter_custom_fusion.2 = bf16[1088]{0:T(1024)(128)(2,1)S(1)} fusion(s32[1024]{0:T(1024)S(1)} %bitcast.54, bf16[1024]{0:T(1024)(128)(2,1)S(1)} %broadcast.149, bf16[]{:T(256)} %constant.63.clone.1), kind=kCustom, calls=%fused_computation.74 | custom fusion | bytes 2178 | tf_op jit(solution)/shard_map/scatter | solution.py:27
  48.0 4.8 gather_fusion
  52.8 3.6 gather.17
  56.4 3.4 broadcast_multiply_fusion
  61.9 6.3 all-to-all-start.2
  68.3 3.8 copy.56
  72.1 35.3 %all-to-all-done.2 = bf16[16,4,17,768]{3,0,2,1:T(8,128)(2,1)S(1)} async-done(((bf16[16,4,17,768]{3,0,2,1:T(8,128)(2,1)}), bf16[16,4,17,768]{3,0,2,1:T(8,128)(2,1)S(1)}, u32[]{:S(2)}, u32[]{:S(2)}) %all-to-all-start.2) | async-done | bytes 1671200 | tf_op jit(solution)/shard_map/all_to_all | solution.py:42
  107.3 3.6 all-to-all-start.1
  111.4 18.8 %all-gather.6.cloned.1.call-done = bf16[16,768,384]{1,2,0:T(8,128)(2,1)} async-done(((bf16[16,768,192]{1,2,0:T(8,128)(2,1)}), bf16[16,768,384]{1,2,0:T(8,128)(2,1)}) %all-gather.6.cloned.1.call-update) | async-done | bytes 9437200 | tf_op jit(solution)/shard_map/all_gather | solution.py:48
  130.2 7.4 convolution_convert_fusion.4
  137.7 112.2 %all-gather.8.cloned.1.call-done = bf16[16,768,384]{1,2,0:T(8,128)(2,1)} async-done(((bf16[16,768,192]{1,2,0:T(8,128)(2,1)}), bf16[16,768,384]{1,2,0:T(8,128)(2,1)}) %all-gather.8.cloned.1.call-update) | async-done | bytes 9437200 | tf_op jit(solution)/shard_map/all_gather | solution.py:47
  249.8 7.5 convolution_convert_fusion.3
  257.3 112.0 %all-gather.4.cloned.1.call-done = bf16[16,384,768]{2,1,0:T(8,128)(2,1)} async-done(((bf16[16,192,768]{2,1,0:T(8,128)(2,1)}), bf16[16,384,768]{2,1,0:T(8,128)(2,1)}) %all-gather.4.cloned.1.call-update) | async-done | bytes 9437200 | tf_op jit(solution)/shard_map/all_gather | solution.py:49
  369.3 7.5 fusion.14
  377.7 4.3 scatter_custom_fusion
  382.3 10.0 %all_to_all.25 = bf16[4,2,136]{2,1,0:T(2,128)(2,1)S(1)} all-to-all(bf16[4,2,136]{2,1,0:T(2,128)(2,1)S(1)} %reshape.281), channel_id=1, replica_groups=mesh['groups'=2,'expert'=4,'dp'=2,'inner'=2] {'expert'}, dimensions={0} | all-to-all | bytes 4352 | tf_op jit(solution)/shard_map/all_to_all | solution.py:44
  392.5 7.0 all-reduce.3.cloned.1.call-done
  399.5 8.3 %convolution_convert_fusion.2 = bf16[16,768,384]{1,2,0:T(8,128)(2,1)} fusion(bf16[16,68,768]{2,0,1:T(8,128)(2,1)S(1)} %bitcast.41, bf16[16,68,384]{2,1,0:T(8,128)(2,1)} %get-tuple-element.21, bf16[16,68,384]{2,1,0:T(8,128)(2,1)} %get-tuple-element.20, bf16[16,68,384]{2,1,0:T(8,128)(2,1)} %get-tuple-element.22, f32[16,68]{1,0:T(8,128)S(1)} %reshape.215), kind=kOutput, calls=%fused_computation.9 | convolution fusion | flops 652296192 | bytes 13619456 | tf_op jit(solution)/shard_map/jrd,jrf->jdf/dot_general | solution.py:100
  408.0 8.2 %convolution_convert_fusion.1 = bf16[16,768,384]{1,2,0:T(8,128)(2,1)} fusion(bf16[16,68,768]{2,0,1:T(8,128)(2,1)S(1)} %bitcast.42, bf16[16,68,384]{2,1,0:T(8,128)(2,1)} %get-tuple-element.20, f32[16,68]{1,0:T(8,128)S(1)} %reshape.215, bf16[16,68,384]{2,1,0:T(8,128)(2,1)} %get-tuple-element.22), kind=kOutput, calls=%fused_computation.8 | convolution fusion | flops 650207232 | bytes 12783872 | tf_op jit(solution)/shard_map/jrd,jrf->jdf/dot_general | solution.py:103
  417.4 7.6 %convolution_convert_fusion = bf16[16,384,768]{2,1,0:T(8,128)(2,1)} fusion(bf16[16,68,768]{2,0,1:T(8,128)(2,1)S(1)} %multiply_convert_fusion, bf16[16,68,384]{2,1,0:T(8,128)(2,1)} %get-tuple-element.21, bf16[16,68,384]{2,1,0:T(8,128)(2,1)S(1)} %copy-done.4), kind=kOutput, calls=%fused_computation.7 | convolution fusion | flops 649789440 | bytes 12779520 | tf_op jit(solution)/shard_map/jrf,jrd->jfd/dot_general | solution.py:105
  429.0 4.8 all-to-all-start.4
  433.9 6.1 fusion.41
  444.1 5.3 all-to-all-start.3
  449.7 6.8 gather_fusion.3
  457.2 31.1 %all-to-all-done.3 = bf16[16,4,17,768]{3,0,2,1:T(8,128)(2,1)S(1)} async-done(((bf16[16,4,17,768]{3,0,2,1:T(8,128)(2,1)}), bf16[16,4,17,768]{3,0,2,1:T(8,128)(2,1)S(1)}, u32[]{:S(2)}, u32[]{:S(2)}) %all-to-all-start.3) | async-done | bytes 1671200 | tf_op jit(solution)/shard_map/all_to_all | solution.py:80
  493.1 4.0 gather_fusion.2
  498.8 20.8 %reduce-scatter.4.cloned.1.call-done = bf16[16,768,192]{1,2,0:T(8,128)(2,1)} async-done(((bf16[16,768,384]{1,2,0:T(8,128)(2,1)}), bf16[16,768,192]{1,2,0:T(8,128)(2,1)}) %reduce-scatter.4.cloned.1.call-update) | async-done | bytes 4718608 | tf_op jit(solution)/shard_map/reduce_scatter | solution.py:107
  519.6 113.3 %reduce-scatter.6.cloned.1.call-done = bf16[16,768,192]{1,2,0:T(8,128)(2,1)} async-done(((bf16[16,768,384]{1,2,0:T(8,128)(2,1)}), bf16[16,768,192]{1,2,0:T(8,128)(2,1)}) %reduce-scatter.6.cloned.1.call-update) | async-done | bytes 4718608 | tf_op jit(solution)/shard_map/reduce_scatter | solution.py:110
  633.0 113.5 %reduce-scatter.8.cloned.1.call-done = bf16[16,192,768]{2,1,0:T(8,128)(2,1)} async-done(((bf16[16,384,768]{2,1,0:T(8,128)(2,1)}), bf16[16,192,768]{2,1,0:T(8,128)(2,1)}) %reduce-scatter.8.cloned.1.call-update) | async-done | bytes 4718608 | tf_op jit(solution)/shard_map/reduce_scatter | solution.py:113
  (83 shorter events, 26.8 us)
Async XLA Ops:
  7.2 25.7 %copy-start = (bf16[128,768]{1,0:T(8,128)(2,1)S(1)}, bf16[128,768]{1,0:T(8,128)(2,1)}, u32[]{:S(2)}) copy-start(bf16[128,768]{1,0:T(8,128)(2,1)} %param.7) | copy-start | bytes 589828
  7.2 123.1 %all-gather.6.cloned.1.call-start = ((), (), s32[]{:S(2)}) async-start(), calls=%async_computation.9 | async-start | bytes 14155776 | tf_op jit(solution)/shard_map/all_gather | solution.py:48
  7.9 241.9 %all-gather.8.cloned.1.call-start = ((), (), s32[]{:S(2)}) async-start(), calls=%async_computation.10 | async-start | bytes 14155776 | tf_op jit(solution)/shard_map/all_gather | solution.py:47
  8.7 0.7 copy-start.5
  8.7 360.6 %all-gather.4.cloned.1.call-start = ((), (), s32[]{:S(2)}) async-start(), calls=%async_computation.8 | async-start | bytes 14155776 | tf_op jit(solution)/shard_map/all_gather | solution.py:49
  37.7 10.3 %copy-start.2 = (bf16[128,768]{1,0:T(8,128)(2,1)S(1)}, bf16[128,768]{1,0:T(8,128)(2,1)}, u32[]{:S(2)}) copy-start(bf16[128,768]{1,0:T(8,128)(2,1)} %param.8) | copy-start | bytes 589828
  61.9 45.4 %all-to-all-start.2 = ((bf16[16,4,17,768]{3,0,2,1:T(8,128)(2,1)}), bf16[16,4,17,768]{3,0,2,1:T(8,128)(2,1)S(1)}, u32[]{:S(2)}, u32[]{:S(2)}) async-start(bf16[16,4,17,768]{3,0,2,1:T(8,128)(2,1)} %copy.58), calls=%async_computation.2 | async-start | bytes 3342336 | tf_op jit(solution)/shard_map/all_to_all | solution.py:42
  107.3 150.0 %all-to-all-start.1 = ((bf16[16,4,17,768]{3,0,2,1:T(8,128)(2,1)}), bf16[16,4,17,768]{3,0,2,1:T(8,128)(2,1)S(1)}, u32[]{:S(2)}, u32[]{:S(2)}) async-start(bf16[16,4,17,768]{3,0,2,1:T(8,128)(2,1)} %copy.56), calls=%async_computation.1 | async-start | bytes 3342336 | tf_op jit(solution)/shard_map/all_to_all | solution.py:43
  110.9 288.5 %all-reduce.3.cloned.1.call-start = ((), (), s32[]{:S(2)}) async-start(), calls=%async_computation.14 | async-start | bytes 5308416 | tf_op jit(solution)/shard_map/psum | solution.py:68
  376.8 0.7 copy-start.6
  376.8 142.8 %reduce-scatter.4.cloned.1.call-start = ((), (), s32[]{:S(2)}) async-start(), calls=%async_computation.11 | async-start | bytes 14155776 | tf_op jit(solution)/shard_map/reduce_scatter | solution.py:107
  407.8 225.2 %reduce-scatter.6.cloned.1.call-start = ((), (), s32[]{:S(2)}) async-start(), calls=%async_computation.12 | async-start | bytes 14155776 | tf_op jit(solution)/shard_map/reduce_scatter | solution.py:110
  416.2 1.2 copy-start.4
  416.2 330.2 %reduce-scatter.8.cloned.1.call-start = ((), (), s32[]{:S(2)}) async-start(), calls=%async_computation.13 | async-start | bytes 14155776 | tf_op jit(solution)/shard_map/reduce_scatter | solution.py:113
  425.0 1.2 copy-start.3
  426.2 13.8 %slice-start = ((s8[9437184]{0:T(1024)(128)(4,1)}), s8[1048576]{0:T(1024)(128)(4,1)S(1)}, s32[]{:S(2)}) async-start(s8[9437184]{0:T(1024)(128)(4,1)} %bitcast.44), calls=%async_computation.15 | async-start | bytes 2097152
  429.0 15.0 %all-to-all-start.4 = ((bf16[4,2,136]{2,1,0:T(2,128)(2,1)}), bf16[4,2,136]{2,1,0:T(2,128)(2,1)S(1)}, u32[]{:S(2)}, u32[]{:S(2)}) async-start(bf16[4,2,136]{2,1,0:T(2,128)(2,1)} %reshape.283), calls=%async_computation.4 | async-start | bytes 8192 | tf_op jit(solution)/shard_map/all_to_all | solution.py:87
  433.9 6.1 slice-start.1
  433.9 6.7 slice-start.2
  444.1 44.2 %all-to-all-start.3 = ((bf16[16,4,17,768]{3,0,2,1:T(8,128)(2,1)}), bf16[16,4,17,768]{3,0,2,1:T(8,128)(2,1)S(1)}, u32[]{:S(2)}, u32[]{:S(2)}) async-start(bf16[16,4,17,768]{3,0,2,1:T(8,128)(2,1)} %bitcast.6), calls=%async_computation.3 | async-start | bytes 3342336 | tf_op jit(solution)/shard_map/all_to_all | solution.py:80
  493.1 253.4 %copy-start.1 = (bf16[128,768]{1,0:T(8,128)(2,1)S(1)}, bf16[128,768]{1,0:T(8,128)(2,1)}, u32[]{:S(2)}) copy-start(bf16[128,768]{1,0:T(8,128)(2,1)} %param.7) | copy-start | bytes 589828
Sparse Core Ops, SparseCore 0:
  9.6 120.6 all-gather.5
  131.8 117.9 all-gather.7
  251.4 117.8 all-gather.3
  376.9 22.4 all-reduce.2
  407.9 111.6 reduce-scatter.3
  522.4 110.5 reduce-scatter.5
  635.9 110.5 reduce-scatter.7
where the time goes:
time: 762 us; the launch traced here: 754 us
  waiting for transfers between devices  566 us (74%)
  local copies, waits for them, and re-layouts  61.4 us (8%)
  matrix products  54.5 us (7%)
  other arithmetic  25.9 us (3%)
  starting transfers between devices  20.9 us (3%)
  between operations  14.7 us (2%)
  blocking collectives  10 us (1%)
    reduce_scatter x1, waiting for transfers between devices, on_device(): lax.psum_scatter(grad_down.astype(jnp.bfloat16), 'dp', scatter_dimension=...  113 us
    reduce_scatter x1, waiting for transfers between devices, on_device(): lax.psum_scatter(grad_up.astype(jnp.bfloat16), 'dp', scatter_dimension=2,...  113 us
    all_gather x1, waiting for transfers between devices, on_device(): lax.all_gather(gate_weight, 'dp', axis=2, tiled=True)  112 us
    all_gather x1, waiting for transfers between devices, on_device(): lax.all_gather(down_weight, 'dp', axis=1, tiled=True)  112 us
    all_to_all x1, waiting for transfers between devices, on_device(): lax.all_to_all(sent_rows, 'expert', split_axis=1, concat_axis=1, tiled=True)  35.3 us
    all_to_all x1, waiting for transfers between devices, on_device(): lax.all_to_all(row_grads.reshape(per_dev, owners, capacity, width_half),...  31.1 us
    reduce_scatter x1, waiting for transfers between devices, on_device(): lax.psum_scatter(grad_gate.astype(jnp.bfloat16), 'dp', scatter_dimension=...  20.8 us
    all_gather x1, waiting for transfers between devices, on_device(): lax.all_gather(up_weight, 'dp', axis=2, tiled=True)  18.8 us
  transfers between devices with their start and end apart: 11, of which 9 were waited for; matrix products, arithmetic and copies ran while one was open for 16% of the time, Pallas kernels for 0%

commit v1 on v0

--- a/solution.py
+++ b/solution.py
@@ -1,7 +1,28 @@
+import functools
 import jax
 import jax.numpy as jnp
 from jax import lax
 from jax.sharding import PartitionSpec as P
+
+
+def press_the_records(q_in, net_axis):
+    t1 = lax.axis_size(net_axis)
+    y = lax.axis_index(net_axis)
+    item_now, row_out = (t1, y)
+    aux, z2 = (q_in, 1)
+    while z2 < item_now:
+        t_next = range(item_now)
+        wide_out = map(lambda jj: (jj, jj ^ z2), t_next)
+        upper = list(wide_out)
+        arr_next = lax.ppermute(aux, net_axis, perm=upper)
+        frame_out = jnp.concatenate([aux, arr_next], axis=2)
+        tmp = jnp.concatenate([arr_next, aux], axis=2)
+        aux = jnp.where(row_out & z2 == 0, frame_out, tmp)
+        z2 = 2 * z2
+    return aux
+
+
+_trace_skins = functools.partial(press_the_records, net_axis="dp")
 
 
 def on_device(tokens, out_grad, expert_ids, gate_probs, gate_weight, up_weight, down_weight):
@@ -44,7 +65,7 @@
         lax.all_to_all(sent_probs, "expert", split_axis=1, concat_axis=1, tiled=True),
     )
     full_gate, full_up, full_down = (
-        lax.all_gather(gate_weight, "dp", axis=2, tiled=True),
+        _trace_skins(gate_weight),
         lax.all_gather(up_weight, "dp", axis=2, tiled=True),
         lax.all_gather(down_weight, "dp", axis=1, tiled=True),
     )

time: 762 us -> 729 us (0.957)
  waiting for transfers between devices: 566 us -> 521 us
  matrix products: 54.5 us -> 67.3 us
    all_gather x1 -> x0, waiting for transfers between devices: 112 us -> none  [on_device(): lax.all_gather(gate_weight, 'dp', axis=2, tiled=True)]
    ppermute x0 -> x1, waiting for transfers between devices: none -> 88.3 us  [press_the_records(): arr_next = lax.ppermute(aux, net_axis, perm=upper)]
    all_gather x1, waiting for transfers between devices: 18.8 us -> 4.68 us  [on_device(): lax.all_gather(up_weight, 'dp', axis=2, tiled=True)]
    reduce_scatter x1, waiting for transfers between devices: 20.8 us -> 12.1 us  [on_device(): lax.psum_scatter(grad_gate.astype(jnp.bfloat16), 'dp', scatter_dimension=...]
  transfers between devices with their start and end apart: 11 -> 11, of which waited for: 9 -> 9; matrix products, arithmetic and copies ran while one was open for 16% -> 19% of each run, Pallas kernels for 0% -> 0%
where the time goes in v1:
time: 729 us; the launch traced here: 720 us
  waiting for transfers between devices  521 us (71%)
  matrix products  67.3 us (9%)
  local copies, waits for them, and re-layouts  59.1 us (8%)
  other arithmetic  25.8 us (4%)
  starting transfers between devices  22.7 us (3%)
  between operations  14.6 us (2%)
  blocking collectives  9.97 us (1%)
    reduce_scatter x1, waiting for transfers between devices, on_device(): lax.psum_scatter(grad_up.astype(jnp.bfloat16), 'dp', scatter_dimension=2,...  113 us
    reduce_scatter x1, waiting for transfers between devices, on_device(): lax.psum_scatter(grad_down.astype(jnp.bfloat16), 'dp', scatter_dimension=...  113 us
    all_gather x1, waiting for transfers between devices, on_device(): lax.all_gather(down_weight, 'dp', axis=1, tiled=True)  113 us
    ppermute x1, waiting for transfers between devices, press_the_records(): arr_next = lax.ppermute(aux, net_axis, perm=upper)  88.3 us
    all_to_all x1, waiting for transfers between devices, on_device(): lax.all_to_all(sent_rows, 'expert', split_axis=1, concat_axis=1, tiled=True)  36.7 us
    all_to_all x1, waiting for transfers between devices, on_device(): lax.all_to_all(row_grads.reshape(per_dev, owners, capacity, width_half),...  31.1 us
    another operation x3, other arithmetic  18.2 us
  transfers between devices with their start and end apart: 11, of which 9 were waited for; matrix products, arithmetic and copies ran while one was open for 19% of the time, Pallas kernels for 0%

profile of v1, /device:TPU:0, one launch (start us, length us, event | category | flops | bytes accessed | tf_op | source)
XLA Modules:
  0.0 720.5 jit_solution(17001487226899987799)
XLA Ops:
  12.1 18.0 %reduce-window.6 = s32[64,8,128]{2,1,0:T(8,128)S(1)} reduce-window(s32[64,8,128]{2,1,0:T(8,128)S(1)} %fusion.26, s32[]{:T(128)} %constant.55.clone.1), window={size=1x1x128 pad=0_0x0_0x127_0}, to_apply=%region_0.0 | reduce-window | flops 8323072 | bytes 524292 | tf_op jit(solution)/shard_map/reduce-window
  30.8 4.3 scatter_custom_fusion.1
  35.1 4.8 gather_fusion.1
  42.5 7.6 %scatter_custom_fusion.2 = bf16[1088]{0:T(1024)(128)(2,1)S(1)} fusion(s32[1024]{0:T(1024)S(1)} %bitcast.46, bf16[1024]{0:T(1024)(128)(2,1)S(1)} %broadcast.155, bf16[]{:T(256)} %constant.67.clone.1), kind=kCustom, calls=%fused_computation.76 | custom fusion | bytes 2178 | tf_op jit(solution)/shard_map/scatter | solution.py:48
  50.2 4.8 gather_fusion
  55.0 3.6 gather.17
  58.6 3.4 broadcast_multiply_fusion
  64.2 5.0 all-to-all-start.2
  71.4 36.7 %all-to-all-done.2 = bf16[16,4,17,768]{3,0,2,1:T(8,128)(2,1)} async-done(((bf16[16,4,17,768]{3,0,2,1:T(8,128)(2,1)}), bf16[16,4,17,768]{3,0,2,1:T(8,128)(2,1)}, u32[]{:S(2)}, u32[]{:S(2)}) %all-to-all-start.2) | async-done | bytes 1671200 | tf_op jit(solution)/shard_map/all_to_all | solution.py:63
  108.1 3.6 all-to-all-start.1
  112.0 88.3 %collective-permute-done = bf16[16,768,192]{1,2,0:T(8,128)(2,1)} collective-permute-done((bf16[16,768,192]{1,2,0:T(8,128)(2,1)}, bf16[16,768,192]{1,2,0:T(8,128)(2,1)}, u32[]{:S(2)}, u32[]{:S(2)}) %collective-permute-start) | collective-permute-done | bytes 4718624 | tf_op jit(solution)/shard_map/ppermute | solution.py:17
  200.3 10.1 %fusion.18 = bf16[16,68,384]{2,1,0:T(8,128)(2,1)} fusion(bf16[16,768,192]{1,2,0:T(8,128)(2,1)} %collective-permute-done, bf16[16,768,192]{1,2,0:T(8,128)(2,1)} %param.11, pred[]{:T(512)S(6)} %eq.38, bf16[16,68,768]{2,0,1:T(8,128)(2,1)} %bitcast.5), kind=kOutput, calls=%fused_computation.38 | convolution fusion | flops 684613632 | bytes 11943937 | tf_op jit(solution)/shard_map/jrd,jdf->jrf/dot_general | solution.py:73
  210.4 4.7 all-gather.5.cloned.1.call-done
  215.1 8.0 %convolution_convert_fusion.3 = bf16[16,68,384]{2,1,0:T(8,128)(2,1)} fusion(bf16[16,768,384]{1,2,0:T(8,128)(2,1)} %all-gather.5.cloned.1.call-done, bf16[16,68,768]{2,0,1:T(8,128)(2,1)} %bitcast.5), kind=kOutput, calls=%fused_computation.37 | convolution fusion | flops 642146304 | bytes 11943936 | tf_op jit(solution)/shard_map/jrd,jdf->jrf/dot_general | solution.py:76
  223.0 113.0 %all-gather.3.cloned.1.call-done = bf16[16,384,768]{2,1,0:T(8,128)(2,1)} async-done(((bf16[16,192,768]{2,1,0:T(8,128)(2,1)}), bf16[16,384,768]{2,1,0:T(8,128)(2,1)}) %all-gather.3.cloned.1.call-update) | async-done | bytes 9437200 | tf_op jit(solution)/shard_map/all_gather | solution.py:70
  336.1 7.4 %fusion.15 = bf16[16,68,384]{2,1,0:T(8,128)(2,1)} fusion(bf16[16,384,768]{2,1,0:T(8,128)(2,1)} %all-gather.3.cloned.1.call-done, bf16[16,68,768]{2,0,1:T(8,128)(2,1)S(1)} %bitcast.37), kind=kOutput, calls=%fused_computation.36 | convolution fusion | flops 642146304 | bytes 11943936 | tf_op jit(solution)/shard_map/jrd,jfd->jrf/dot_general | solution.py:86
  344.4 4.3 scatter_custom_fusion
  349.0 10.0 %all_to_all.25 = bf16[4,2,136]{2,1,0:T(2,128)(2,1)S(1)} all-to-all(bf16[4,2,136]{2,1,0:T(2,128)(2,1)S(1)} %reshape.281), channel_id=1, replica_groups=mesh['groups'=2,'expert'=4,'dp'=2,'inner'=2] {'expert'}, dimensions={0} | all-to-all | bytes 4352 | tf_op jit(solution)/shard_map/all_to_all | solution.py:65
  359.2 7.0 all-reduce.3.cloned.1.call-done
  366.1 8.8 %convolution_convert_fusion.2 = bf16[16,768,384]{1,2,0:T(8,128)(2,1)} fusion(bf16[16,68,768]{2,0,1:T(8,128)(2,1)} %bitcast.5, bf16[16,68,384]{2,1,0:T(8,128)(2,1)} %get-tuple-element.21, bf16[16,68,384]{2,1,0:T(8,128)(2,1)} %get-tuple-element.20, bf16[16,68,384]{2,1,0:T(8,128)(2,1)} %get-tuple-element.22, f32[16,68]{1,0:T(8,128)S(1)} %reshape.215), kind=kOutput, calls=%fused_computation.10 | convolution fusion | flops 652296192 | bytes 13619456 | tf_op jit(solution)/shard_map/jrd,jrf->jdf/dot_general | solution.py:121
  376.1 8.4 %convolution_convert_fusion.1 = bf16[16,768,384]{1,2,0:T(8,128)(2,1)} fusion(bf16[16,68,768]{2,0,1:T(8,128)(2,1)} %bitcast.5, bf16[16,68,384]{2,1,0:T(8,128)(2,1)S(1)} %copy-done.4, f32[16,68]{1,0:T(8,128)S(1)} %reshape.215, bf16[16,68,384]{2,1,0:T(8,128)(2,1)} %get-tuple-element.22), kind=kOutput, calls=%fused_computation.9 | convolution fusion | flops 650207232 | bytes 12783872 | tf_op jit(solution)/shard_map/jrd,jrf->jdf/dot_general | solution.py:124
  385.0 7.9 %convolution_convert_fusion = bf16[16,384,768]{2,1,0:T(8,128)(2,1)} fusion(bf16[16,68,768]{2,0,1:T(8,128)(2,1)S(1)} %multiply_convert_fusion, bf16[16,68,384]{2,1,0:T(8,128)(2,1)} %get-tuple-element.21, bf16[16,68,384]{2,1,0:T(8,128)(2,1)} %get-tuple-element.22), kind=kOutput, calls=%fused_computation.8 | convolution fusion | flops 649789440 | bytes 12779520 | tf_op jit(solution)/shard_map/jrf,jrd->jfd/dot_general | solution.py:126
  396.8 4.8 all-to-all-start.4
  401.7 6.2 fusion.43
  407.8 10.5 %add_convert_fusion = bf16[16,68,768]{2,1,0:T(8,128)(2,1)S(1)} fusion(f32[16,68,768]{2,1,0:T(8,128)S(1)} %fusion.43, bf16[16,768,192]{1,2,0:T(8,128)(2,1)} %collective-permute-done, bf16[16,768,192]{1,2,0:T(8,128)(2,1)} %param.11, pred[]{:T(512)S(6)} %eq.38, bf16[16,68,384]{2,1,0:T(8,128)(2,1)S(1)} %copy-done.5, bf16[16,68,384]{2,1,0:T(8,128)(2,1)S(1)} %copy-done.4, ...), kind=kOutput, calls=%fused_computation.11 | convolution fusion | flops 691716096 | bytes 16961792 | tf_op jit(solution)/shard_map/jrf,jdf->jrd/dot_general | solution.py:96
  419.9 5.3 all-to-all-start.3
  425.5 6.8 gather_fusion.3
  433.0 31.1 %all-to-all-done.3 = bf16[16,4,17,768]{3,0,2,1:T(8,128)(2,1)S(1)} async-done(((bf16[16,4,17,768]{3,0,2,1:T(8,128)(2,1)}), bf16[16,4,17,768]{3,0,2,1:T(8,128)(2,1)S(1)}, u32[]{:S(2)}, u32[]{:S(2)}) %all-to-all-start.3) | async-done | bytes 1671200 | tf_op jit(solution)/shard_map/all_to_all | solution.py:101
  468.9 4.0 gather_fusion.2
  474.7 12.1 %reduce-scatter.4.cloned.1.call-done = bf16[16,768,192]{1,2,0:T(8,128)(2,1)} async-done(((bf16[16,768,384]{1,2,0:T(8,128)(2,1)}), bf16[16,768,192]{1,2,0:T(8,128)(2,1)}) %reduce-scatter.4.cloned.1.call-update) | async-done | bytes 4718608 | tf_op jit(solution)/shard_map/reduce_scatter | solution.py:128
  486.8 113.3 %reduce-scatter.6.cloned.1.call-done = bf16[16,768,192]{1,2,0:T(8,128)(2,1)} async-done(((bf16[16,768,384]{1,2,0:T(8,128)(2,1)}), bf16[16,768,192]{1,2,0:T(8,128)(2,1)}) %reduce-scatter.6.cloned.1.call-update) | async-done | bytes 4718608 | tf_op jit(solution)/shard_map/reduce_scatter | solution.py:131
  600.1 113.3 %reduce-scatter.8.cloned.1.call-done = bf16[16,192,768]{2,1,0:T(8,128)(2,1)} async-done(((bf16[16,384,768]{2,1,0:T(8,128)(2,1)}), bf16[16,192,768]{2,1,0:T(8,128)(2,1)}) %reduce-scatter.8.cloned.1.call-update) | async-done | bytes 4718608 | tf_op jit(solution)/shard_map/reduce_scatter | solution.py:134
  (79 shorter events, 28.7 us)
Async XLA Ops:
  7.2 28.0 %copy-start = (bf16[128,768]{1,0:T(8,128)(2,1)S(1)}, bf16[128,768]{1,0:T(8,128)(2,1)}, u32[]{:S(2)}) copy-start(bf16[128,768]{1,0:T(8,128)(2,1)} %param.7) | copy-start | bytes 589828
  7.2 207.9 %all-gather.5.cloned.1.call-start = ((), (), s32[]{:S(2)}) async-start(), calls=%async_computation.9 | async-start | bytes 14155776 | tf_op jit(solution)/shard_map/all_gather | solution.py:69
  7.9 3.8 copy-start.7
  7.9 328.2 %all-gather.3.cloned.1.call-start = ((), (), s32[]{:S(2)}) async-start(), calls=%async_computation.8 | async-start | bytes 14155776 | tf_op jit(solution)/shard_map/all_gather | solution.py:70
  8.7 191.6 %collective-permute-start = (bf16[16,768,192]{1,2,0:T(8,128)(2,1)}, bf16[16,768,192]{1,2,0:T(8,128)(2,1)}, u32[]{:S(2)}, u32[]{:S(2)}) collective-permute-start(bf16[16,768,192]{1,2,0:T(8,128)(2,1)} %param.11), channel_id=1, source_target_pairs={{0,2},{2,0},{1,3},{3,1},{4,6},{6,4},{5,7},{7,5},{8,10},{10,8},{9,1... | collective-permute-start | bytes 14155784 | tf_op jit(solution)/shard_map/ppermute | solution.py:17
  39.9 10.3 %copy-start.2 = (bf16[128,768]{1,0:T(8,128)(2,1)S(1)}, bf16[128,768]{1,0:T(8,128)(2,1)}, u32[]{:S(2)}) copy-start(bf16[128,768]{1,0:T(8,128)(2,1)} %param.8) | copy-start | bytes 589828
  64.2 5.0 copy-start.3
  64.2 43.9 %all-to-all-start.2 = ((bf16[16,4,17,768]{3,0,2,1:T(8,128)(2,1)}), bf16[16,4,17,768]{3,0,2,1:T(8,128)(2,1)}, u32[]{:S(2)}, u32[]{:S(2)}) async-start(bf16[16,4,17,768]{3,0,2,1:T(8,128)(2,1)} %copy.64), calls=%async_computation.2 | async-start | bytes 3342336 | tf_op jit(solution)/shard_map/all_to_all | solution.py:63
  108.1 114.9 %all-to-all-start.1 = ((bf16[16,4,17,768]{3,0,2,1:T(8,128)(2,1)}), bf16[16,4,17,768]{3,0,2,1:T(8,128)(2,1)S(1)}, u32[]{:S(2)}, u32[]{:S(2)}) async-start(bf16[16,4,17,768]{3,0,2,1:T(8,128)(2,1)} %copy.62), calls=%async_computation.1 | async-start | bytes 3342336 | tf_op jit(solution)/shard_map/all_to_all | solution.py:64
  111.7 254.5 %all-reduce.3.cloned.1.call-start = ((), (), s32[]{:S(2)}) async-start(), calls=%async_computation.13 | async-start | bytes 5308416 | tf_op jit(solution)/shard_map/psum | solution.py:89
  343.5 0.7 copy-start.8
  343.5 143.2 %reduce-scatter.4.cloned.1.call-start = ((), (), s32[]{:S(2)}) async-start(), calls=%async_computation.10 | async-start | bytes 14155776 | tf_op jit(solution)/shard_map/reduce_scatter | solution.py:128
  374.9 1.2 copy-start.4
  374.9 225.2 %reduce-scatter.6.cloned.1.call-start = ((), (), s32[]{:S(2)}) async-start(), calls=%async_computation.11 | async-start | bytes 14155776 | tf_op jit(solution)/shard_map/reduce_scatter | solution.py:131
  384.5 328.9 %reduce-scatter.8.cloned.1.call-start = ((), (), s32[]{:S(2)}) async-start(), calls=%async_computation.12 | async-start | bytes 14155776 | tf_op jit(solution)/shard_map/reduce_scatter | solution.py:134
  392.9 1.2 copy-start.5
  396.8 23.1 %all-to-all-start.4 = ((bf16[4,2,136]{2,1,0:T(2,128)(2,1)}), bf16[4,2,136]{2,1,0:T(2,128)(2,1)S(1)}, u32[]{:S(2)}, u32[]{:S(2)}) async-start(bf16[4,2,136]{2,1,0:T(2,128)(2,1)} %reshape.283), calls=%async_computation.4 | async-start | bytes 8192 | tf_op jit(solution)/shard_map/all_to_all | solution.py:108
  401.7 6.2 copy-start.6
  419.9 44.3 %all-to-all-start.3 = ((bf16[16,4,17,768]{3,0,2,1:T(8,128)(2,1)}), bf16[16,4,17,768]{3,0,2,1:T(8,128)(2,1)S(1)}, u32[]{:S(2)}, u32[]{:S(2)}) async-start(bf16[16,4,17,768]{3,0,2,1:T(8,128)(2,1)} %bitcast.6), calls=%async_computation.3 | async-start | bytes 3342336 | tf_op jit(solution)/shard_map/all_to_all | solution.py:101
  468.9 244.5 %copy-start.1 = (bf16[128,768]{1,0:T(8,128)(2,1)S(1)}, bf16[128,768]{1,0:T(8,128)(2,1)}, u32[]{:S(2)}) copy-start(bf16[128,768]{1,0:T(8,128)(2,1)} %param.7) | copy-start | bytes 589828
Sparse Core Ops, SparseCore 0:
  9.6 205.4 all-gather.4
  216.6 119.4 all-gather.2
  343.7 22.4 all-reduce.2
  375.1 111.6 reduce-scatter.3
  489.5 110.5 reduce-scatter.5
  602.8 110.5 reduce-scatter.7
